TPU v7x, 32 devices: a whole 2x2x4 slice. The times are simulated.
32 devices in a mesh: shard: 4 (over z), ctx: 4 (over x, core), tp: 2 (over y).
Axes of the slice: x: 2, y: 2, z: 4, core: 2. Of those that a mesh axis runs over, the one named last changes fastest.
Arguments:
- hidden_in: bfloat16 [4, 1024, 1024], P('shard', 'ctx'), may hold values from -6 to 6
- out_grad: bfloat16 [4, 1024, 1024], P('shard', 'ctx'), may hold values from -6 to 6
- segment_ids: int32 [4, 1024], P('shard'), may hold values from 0 to 3, never falling along the last dimension, each value on 1 to 512 neighbouring positions
- w_qkv: bfloat16 [3, 1024, 1024], P(None, 'shard', 'tp'), may hold values from -0.1875 to 0.1875
- bias_qv: float32 [2, 1024], P(None, 'tp'), may hold values from -3 to 3
- w_out: bfloat16 [1024, 1024], P('tp', 'shard'), may hold values from -0.75 to 0.75
- bias_out: float32 [1024], replicated, may hold values from -3 to 3
- norm1_gain: float32 [1024], replicated, may hold values from 0.5 to 1.5
- norm1_shift: float32 [1024], replicated, may hold values from -3 to 3
- w_up: bfloat16 [1024, 4096], P('shard', 'tp'), may hold values from -0.1875 to 0.1875
- bias_up: float32 [4096], P('tp'), may hold values from -3 to 3
- w_down: bfloat16 [4096, 1024], P('tp', 'shard'), may hold values from -0.09375 to 0.09375
- bias_down: float32 [1024], replicated, may hold values from -3 to 3
- norm2_gain: float32 [1024], replicated, may hold values from 0.5 to 1.5
- norm2_shift: float32 [1024], replicated, may hold values from -3 to 3
Outputs:
- output: bfloat16 [4, 1024, 1024], P('shard', 'ctx')
- input_grad: bfloat16 [4, 1024, 1024], P('shard', 'ctx')
- w_qkv_grad: float32 [3, 1024, 1024], P(None, 'shard', 'tp')
- bias_qv_grad: float32 [2, 1024], P(None, 'tp')
- w_out_grad: float32 [1024, 1024], P('tp', 'shard')
- bias_out_grad: float32 [1024], replicated
- norm1_gain_grad: float32 [1024], replicated
- norm1_shift_grad: float32 [1024], replicated
- w_up_grad: float32 [1024, 4096], P('shard', 'tp')
- bias_up_grad: float32 [4096], P('tp')
- w_down_grad: float32 [4096, 1024], P('tp', 'shard')
- bias_down_grad: float32 [1024], replicated
- norm2_gain_grad: float32 [1024], replicated
- norm2_shift_grad: float32 [1024], replicated
Inputs may be any that keep to these rules, and one draw needn't show every extreme that they name: `segment_ids`: within each sequence the ids never fall and start at 0; each document has at most 512 tokens, and some document has exactly that many.
All inputs are finite; a program needn't handle non-finite values.
Results may differ from a plain program's by a relative error of at most 0.022.
The roundings to bfloat16 on the way count: a program that leaves them out, or rounds other values in their place, can miss the bound.
Values may be sent and summed in bfloat16 or wider, within the bound.
A program may use at most 128 MiB of HBM per device.

v0:
```python
import math
import jax
import jax.numpy as jnp
from jax import lax
from jax.sharding import PartitionSpec as P

HEADS = 16
EPSILON = 1e-05


def normalize(resid, gain, shift):
    average = jnp.mean(resid, axis=-1, keepdims=True)
    centred = resid - average
    variance = jnp.mean(centred * centred, axis=-1, keepdims=True)
    inv_std = lax.rsqrt(variance + EPSILON)
    normed = centred * inv_std
    return (normed * gain + shift, normed, inv_std)


def normalize_back(cotan, normed, inv_std, gain):
    scaled = cotan * gain
    return inv_std * (
        scaled
        - jnp.mean(scaled, axis=-1, keepdims=True)
        - normed * jnp.mean(scaled * normed, axis=-1, keepdims=True)
    )


def gelu_value(pre_act):
    return 0.5 * pre_act * (1.0 + jax.scipy.special.erf(pre_act * 0.7071067811865476))


def gelu_slope(pre_act):
    return (
        0.5 * (1.0 + jax.scipy.special.erf(pre_act * 0.7071067811865476))
        + pre_act * jnp.exp(-0.5 * pre_act * pre_act) * 0.3989422804014327
    )


def block_scores(query_block, keys, ids_block, ids_whole, scale):
    scores = (
        jnp.einsum("qhe,khe->hqk", query_block, keys, preferred_element_type=jnp.float32) * scale
    )
    return jnp.where((ids_block[:, None] == ids_whole[None, :])[None], scores, -jnp.inf)


GROUP = ("ctx", "tp")


def dot_t(left, right):
    return lax.dot_general(
        left, right, (((1,), (1,)), ((), ())), preferred_element_type=jnp.float32
    )


def dot_rows(left, right):
    return lax.dot_general(
        left, right, (((0,), (0,)), ((), ())), preferred_element_type=jnp.float32
    )


def dot(left, right):
    return jnp.dot(left, right, preferred_element_type=jnp.float32)


def spread(part):
    return lax.all_gather(part, GROUP, axis=1, tiled=True)


def collect(whole):
    return lax.psum_scatter(whole, GROUP, scatter_dimension=1, tiled=True).astype(jnp.float32)


def shards(
    hidden_in,
    out_grad,
    segment_ids,
    w_qkv,
    bias_qv,
    w_out,
    bias_out,
    norm1_gain,
    norm1_shift,
    w_up,
    bias_up,
    w_down,
    bias_down,
    norm2_gain,
    norm2_shift,
):
    seq_count, local_len, width = hidden_in.shape
    ctx_count = lax.axis_size("ctx")
    tp_count = lax.axis_size("tp")
    ctx_at = lax.axis_index("ctx")
    tp_at = lax.axis_index("tp")
    full_len = local_len * ctx_count
    part_len = local_len // tp_count
    row_count = seq_count * full_len
    head_dim = width // HEADS
    scale = 1.0 / math.sqrt(head_dim)
    owned_rows = w_up.shape[0]
    cols = w_qkv.shape[2] // ctx_count
    units = w_up.shape[1] // ctx_count
    local_heads = cols // head_dim
    block_rows = min(512, full_len)
    block_count = full_len // block_rows

    def mine(array, size, axis):
        return lax.dynamic_slice_in_dim(array, ctx_at * size, size, axis)

    qkv_own = mine(w_qkv, cols, 2).transpose(1, 0, 2).reshape(owned_rows, 3 * cols)
    qkv_full = lax.all_gather(qkv_own, "shard", axis=0, tiled=True)
    tokens_all = lax.all_gather(hidden_in, "ctx", axis=1, tiled=True).reshape(row_count, width)
    rest_own = jnp.concatenate(
        [mine(w_out, cols, 0).T, mine(w_up, units, 1), mine(w_down, units, 0).T], axis=1
    )
    rest_full = lax.all_gather(rest_own, "shard", axis=0, tiled=True)
    out_full = rest_full[:, :cols]
    up_full = rest_full[:, cols : cols + units]
    down_full = rest_full[:, cols + units :]
    bias_own = mine(bias_qv, cols, 1)
    bias_three = jnp.concatenate([bias_own[0], jnp.zeros_like(bias_own[0]), bias_own[1]])
    project = (dot(tokens_all, qkv_full) + bias_three).astype(jnp.bfloat16)
    heads = project.reshape(seq_count, full_len, 3, local_heads, head_dim)

    def attend_sequence(packed):
        seq_heads, seq_ids = packed
        keys = seq_heads[:, 1]
        values = seq_heads[:, 2]
        queries = seq_heads[:, 0].reshape(block_count, block_rows, local_heads, head_dim)
        id_blocks = seq_ids.reshape(block_count, block_rows)

        def attend_block(piece):
            query_block, ids_block = piece
            scores = block_scores(query_block, keys, ids_block, seq_ids, scale)
            log_total = jax.nn.logsumexp(scores, axis=-1)
            probs_low = jnp.exp(scores - log_total[..., None]).astype(jnp.bfloat16)
            attended = jnp.einsum(
                "hqk,khe->qhe", probs_low, values, preferred_element_type=jnp.float32
            ).astype(jnp.bfloat16)
            return (attended, log_total)

        attended, log_total = lax.map(attend_block, (queries, id_blocks))
        return (attended.reshape(full_len, local_heads, head_dim), log_total)

    attended_heads, log_totals = lax.map(attend_sequence, (heads, segment_ids))
    attended = attended_heads.reshape(row_count, cols)

    def whole(part):
        return part.astype(jnp.bfloat16).reshape(seq_count, full_len, width)

    def part_of(array):
        return lax.dynamic_slice_in_dim(array, tp_at * part_len, part_len, 1)

    resid_one = (
        collect(whole(dot_t(attended, out_full)))
        + bias_out
        + part_of(hidden_in).astype(jnp.float32)
    )
    first, normed_one, inv_one = normalize(resid_one, norm1_gain, norm1_shift)
    first_all = spread(first.astype(jnp.bfloat16)).reshape(row_count, width)
    pre_act = dot(first_all, up_full) + mine(bias_up, units, 0)
    activated = gelu_value(pre_act).astype(jnp.bfloat16)
    resid_two = collect(whole(dot_t(activated, down_full))) + bias_down + first
    result, normed_two, inv_two = normalize(resid_two, norm2_gain, norm2_shift)
    grad_float = part_of(out_grad).astype(jnp.float32)

    def total(array):
        return jnp.sum(array, axis=(0, 1))

    gain_two_grad = total(grad_float * normed_two)
    shift_two_grad = total(grad_float)
    resid_two_grad = normalize_back(grad_float, normed_two, inv_two, norm2_gain)
    two_all = spread(resid_two_grad.astype(jnp.bfloat16)).reshape(row_count, width)
    output = lax.all_gather(result.astype(jnp.bfloat16), "tp", axis=1, tiled=True)
    bias_down_grad = total(resid_two_grad)
    pre_grad = dot(two_all, down_full) * gelu_slope(pre_act)
    pre_low = pre_grad.astype(jnp.bfloat16)
    bias_up_grad = jnp.sum(pre_grad, axis=0)
    first_grad = resid_two_grad + collect(whole(dot_t(pre_low, up_full)))
    part_ffn = jnp.concatenate(
        [dot_rows(first_all, pre_low), dot_rows(two_all, activated)], axis=1
    ).astype(jnp.bfloat16)
    gain_one_grad = total(first_grad * normed_one)
    shift_one_grad = total(first_grad)
    resid_one_grad = normalize_back(first_grad, normed_one, inv_one, norm1_gain)
    bias_out_grad = total(resid_one_grad)
    one_all = spread(resid_one_grad.astype(jnp.bfloat16)).reshape(row_count, width)
    attended_grad = dot(one_all, out_full).astype(jnp.bfloat16)
    grad_heads = attended_grad.reshape(seq_count, full_len, local_heads, head_dim)

    def back_sequence(packed):
        seq_heads, seq_ids, seq_attended, seq_grad, seq_log = packed
        keys = seq_heads[:, 1]
        values = seq_heads[:, 2]
        queries = seq_heads[:, 0].reshape(block_count, block_rows, local_heads, head_dim)
        id_blocks = seq_ids.reshape(block_count, block_rows)
        att_blocks = seq_attended.reshape(block_count, block_rows, local_heads, head_dim)
        grad_blocks = seq_grad.reshape(block_count, block_rows, local_heads, head_dim)

        def back_block(carry, piece):
            key_total, value_total = carry
            query_block, ids_block, att_block, grad_block, log_block = piece
            scores = block_scores(query_block, keys, ids_block, seq_ids, scale)
            probs = jnp.exp(scores - log_block[..., None])
            probs_low = probs.astype(jnp.bfloat16)
            prob_grad = jnp.einsum(
                "qhe,khe->hqk", grad_block, values, preferred_element_type=jnp.float32
            )
            offset = jnp.sum(
                grad_block.astype(jnp.float32) * att_block.astype(jnp.float32), axis=-1
            ).T
            score_grad = (probs * (prob_grad - offset[..., None]) * scale).astype(jnp.bfloat16)
            query_grad = jnp.einsum(
                "hqk,khe->qhe", score_grad, keys, preferred_element_type=jnp.float32
            ).astype(jnp.bfloat16)
            key_total = key_total + jnp.einsum(
                "hqk,qhe->khe", score_grad, query_block, preferred_element_type=jnp.float32
            )
            value_total = value_total + jnp.einsum(
                "hqk,qhe->khe", probs_low, grad_block, preferred_element_type=jnp.float32
            )
            return ((key_total, value_total), query_grad)

        empty = jnp.zeros((full_len, local_heads, head_dim), jnp.float32)
        (key_total, value_total), query_grads = lax.scan(
            back_block, (empty, empty), (queries, id_blocks, att_blocks, grad_blocks, seq_log)
        )
        return jnp.stack(
            [
                query_grads.reshape(full_len, local_heads, head_dim),
                key_total.astype(jnp.bfloat16),
                value_total.astype(jnp.bfloat16),
            ],
            axis=1,
        )

    head_grads = lax.map(
        back_sequence, (heads, segment_ids, attended_heads, grad_heads, log_totals)
    )
    proj_grad = head_grads.reshape(row_count, 3 * cols)
    proj_sum = jnp.sum(proj_grad.astype(jnp.float32), axis=0)
    bias_qv_grad = jnp.concatenate([proj_sum[:cols], proj_sum[2 * cols :]])
    input_part = resid_one_grad + collect(whole(dot_t(proj_grad, qkv_full)))
    input_grad = lax.all_gather(input_part.astype(jnp.bfloat16), "tp", axis=1, tiled=True)
    part_attn = jnp.concatenate(
        [dot_rows(tokens_all, proj_grad), dot_rows(one_all, attended)], axis=1
    ).astype(jnp.bfloat16)

    def owned(part):
        mean = lax.psum_scatter(part, "shard", scatter_dimension=0, tiled=True)
        return lax.all_gather(mean, "ctx", axis=0).astype(jnp.float32)

    own_ffn = owned(part_ffn)
    own_attn = owned(part_attn)
    up_grad = own_ffn[:, :, :units].transpose(1, 0, 2).reshape(w_up.shape)
    down_grad = own_ffn[:, :, units:].transpose(0, 2, 1).reshape(w_down.shape)
    qkv_grad = (
        own_attn[:, :, : 3 * cols]
        .reshape(ctx_count, owned_rows, 3, cols)
        .transpose(2, 1, 0, 3)
        .reshape(w_qkv.shape)
    )
    out_weight_grad = own_attn[:, :, 3 * cols :].transpose(0, 2, 1).reshape(w_out.shape)
    sliced = jnp.concatenate([bias_qv_grad, bias_up_grad])
    slots = jnp.zeros((tp_count, ctx_count, sliced.shape[0]), jnp.float32)
    slots = lax.dynamic_update_slice(slots, sliced[None, None], (tp_at, ctx_at, 0))
    small = lax.psum(
        jnp.concatenate(
            [
                bias_out_grad,
                gain_one_grad,
                shift_one_grad,
                bias_down_grad,
                gain_two_grad,
                shift_two_grad,
                slots.reshape(-1),
            ]
        ),
        ("shard", "ctx", "tp"),
    )
    sums = small[: 6 * width].reshape(6, width)
    slots = small[6 * width :].reshape(tp_count, ctx_count, -1)
    slots = lax.dynamic_index_in_dim(slots, tp_at, 0, keepdims=False)
    bias_qv_total = (
        slots[:, : 2 * cols].reshape(ctx_count, 2, cols).transpose(1, 0, 2).reshape(bias_qv.shape)
    )
    return (
        output,
        input_grad,
        qkv_grad,
        bias_qv_total,
        out_weight_grad,
        sums[0],
        sums[1],
        sums[2],
        up_grad,
        slots[:, 2 * cols :].reshape(bias_up.shape),
        down_grad,
        sums[3],
        sums[4],
        sums[5],
    )


def solution(mesh):
    return jax.shard_map(
        shards,
        mesh=mesh,
        in_specs=(
            P("shard", "ctx", None),
            P("shard", "ctx", None),
            P("shard", None),
            P(None, "shard", "tp"),
            P(None, "tp"),
            P("tp", "shard"),
            P(),
            P(),
            P(),
            P("shard", "tp"),
            P("tp"),
            P("tp", "shard"),
            P(),
            P(),
            P(),
        ),
        out_specs=(
            P("shard", "ctx", None),
            P("shard", "ctx", None),
            P(None, "shard", "tp"),
            P(None, "tp"),
            P("tp", "shard"),
            P(),
            P(),
            P(),
            P("shard", "tp"),
            P("tp"),
            P("tp", "shard"),
            P(),
            P(),
            P(),
        ),
        check_vma=False,
    )
```

profile of v0, /device:TPU:0, one launch (start us, length us, event | category | flops | bytes accessed | tf_op | source)
XLA Modules:
  0.0 506.4 jit_solution(6332370861797403989)
XLA Ops:
  14.3 21.3 %all_gather.36 = bf16[1024,384]{0,1:T(8,128)(2,1)S(1)} all-gather(bf16[256,384]{0,1:T(8,128)(2,1)S(1)} %bitcast.238), channel_id=1, replica_groups=mesh['shard'=4,'ctx'=4,'tp'=2] {'shard'}, dimensions={0}, use_global_device_ids=true | all-gather | bytes 983040 | tf_op jit(solution)/shard_map/all_gather | solution.py:112
  35.7 2.6 add_convert_fusion
  38.6 7.9 %while.45 = (s32[]{:T(128)}, bf16[2,512,2,64]{1,3,2,0:T(8,128)(2,1)S(1)}, f32[2,2,512]{2,1,0:T(2,128)S(1)}, s32[2,512]{1,0:T(2,128)S(1)}, s32[1024]{0:T(1024)S(1...) while((s32[]{:T(128)}, ...), condition=%wide.region_3.4_spmd, body=%wide.region_0.3_spmd.sunk | while | flops 280567808 | bytes 15526005 | solution.py:143
  46.8 40.8 %all-gather.12.cloned.1.call-done = bf16[1024,1152]{0,1:T(8,128)(2,1)} async-done(((bf16[256,1152]{0,1:T(8,128)(2,1)}), bf16[1024,1152]{0,1:T(8,128)(2,1)}) %all-gather.12.cloned.1.call-update) | async-done | bytes 2359312 | tf_op jit(solution)/shard_map/all_gather | solution.py:117
  87.6 3.1 convert_bitcast_fusion.3
  90.8 40.0 %reduce-scatter.7.cloned.1.call-done = bf16[1,128,1024]{2,1,0:T(8,128)(2,1)} async-done(((bf16[1,1024,1024]{2,1,0:T(8,128)(2,1)}), bf16[1,128,1024]{2,1,0:T(8,128)(2,1)}) %reduce-scatter.7.cloned.1.call-update) | async-done | bytes 262160 | tf_op jit(solution)/shard_map/reduce_scatter | solution.py:71
  135.8 27.1 %all-gather.14.cloned.1.call-done = bf16[1,1024,1024]{2,1,0:T(8,128)(2,1)} async-done(((bf16[1,128,1024]{2,1,0:T(8,128)(2,1)}), bf16[1,1024,1024]{2,1,0:T(8,128)(2,1)}) %all-gather.14.cloned.1.call-update) | async-done | bytes 2097168 | tf_op jit(solution)/shard_map/all_gather | solution.py:67
  162.9 4.6 multiply_convert_fusion.1
  168.4 3.8 convert_bitcast_fusion.2
  172.3 41.2 %reduce-scatter.9.cloned.1.call-done = bf16[1,128,1024]{2,1,0:T(8,128)(2,1)} async-done(((bf16[1,1024,1024]{2,1,0:T(8,128)(2,1)}), bf16[1,128,1024]{2,1,0:T(8,128)(2,1)}) %reduce-scatter.9.cloned.1.call-update) | async-done | bytes 262160 | tf_op jit(solution)/shard_map/reduce_scatter | solution.py:71
  216.6 27.7 %all-gather.16.cloned.1.call-done = bf16[1,1024,1024]{2,1,0:T(8,128)(2,1)} async-done(((bf16[1,128,1024]{2,1,0:T(8,128)(2,1)}), bf16[1,1024,1024]{2,1,0:T(8,128)(2,1)}) %all-gather.16.cloned.1.call-update) | async-done | bytes 2097168 | tf_op jit(solution)/shard_map/all_gather | solution.py:67
  244.3 4.5 fusion.111
  249.8 3.8 convert_bitcast_fusion.1
  253.7 41.2 %reduce-scatter.11.cloned.1.call-done = bf16[1,128,1024]{2,1,0:T(8,128)(2,1)} async-done(((bf16[1,1024,1024]{2,1,0:T(8,128)(2,1)}), bf16[1,128,1024]{2,1,0:T(8,128)(2,1)}) %reduce-scatter.11.cloned.1.call-update) | async-done | bytes 262160 | tf_op jit(solution)/shard_map/reduce_scatter | solution.py:71
  299.1 3.3 fusion.72
  305.5 21.4 %all-gather.18.cloned.1.call-done = bf16[1,1024,1024]{2,1,0:T(8,128)(2,1)} async-done(((bf16[1,128,1024]{2,1,0:T(8,128)(2,1)}), bf16[1,1024,1024]{2,1,0:T(8,128)(2,1)}) %all-gather.18.cloned.1.call-update) | async-done | bytes 2097168 | tf_op jit(solution)/shard_map/all_gather | solution.py:67
  326.9 2.3 fusion.81
  329.9 12.5 %while.46 = (s32[]{:T(128)}, f32[1024,2,64]{0,2,1:T(8,128)S(1)}, f32[1024,2,64]{0,2,1:T(8,128)}, bf16[2,512,2,64]{1,3,2,0:T(8,128)(2,1)S(1)}, bf16[2,512,2,64]{1...) while((s32[]{:T(128)}, f32[1024,2,64]{0,2,1:T(8,128)S(1)}, ...), condition=%wide.region_17.18_spmd.clone, body=%wide.region_15.17_spmd.clone.sunk | while | flops 683998208 | bytes 29526284 | solution.py:226
  344.2 2.2 fusion.84
  348.4 25.0 %reduce-scatter.17.cloned.1.call-done = bf16[256,1024]{0,1:T(8,128)(2,1)} async-done(((bf16[1024,1024]{0,1:T(8,128)(2,1)}), bf16[256,1024]{0,1:T(8,128)(2,1)}) %reduce-scatter.17.cloned.1.call-update) | async-done | bytes 524304 | tf_op jit(solution)/shard_map/reduce_scatter | solution.py:251
  373.5 2.6 convert_bitcast_fusion
  376.2 8.4 %all_gather.40 = bf16[1,256,1024]{2,1,0:T(8,128)(2,1)} all-gather(bf16[1,128,1024]{2,1,0:T(8,128)(2,1)S(1)} %get-tuple-element.297), channel_id=1, replica_groups=mesh['shard'=4,'ctx'=4,'tp'=2] {'tp'}, dimensions={1}, use_global_device_ids=true | all-gather | bytes 786432 | tf_op jit(solution)/shard_map/all_gather | solution.py:175
  385.0 17.8 %reduce-scatter.15.cloned.1.call-done = bf16[256,512]{0,1:T(8,128)(2,1)} async-done(((bf16[1024,512]{0,1:T(8,128)(2,1)}), bf16[256,512]{0,1:T(8,128)(2,1)}) %reduce-scatter.15.cloned.1.call-update) | async-done | bytes 262160 | tf_op jit(solution)/shard_map/reduce_scatter | solution.py:251
  402.8 39.6 %psum.7 = f32[12288]{0:T(1024)S(1)} all-reduce(f32[12288]{0:T(1024)S(1)} %constant_dynamic-update-slice_fusion), channel_id=1, replica_groups=mesh['shard'=4,'ctx'=4,'tp'=2] {'shard','ctx','tp'}, use_global_device_ids=true, to_apply=%region_28.29 | all-reduce | flops 12288 | bytes 98304 | tf_op jit(solution)/shard_map/psum | solution.py:268
  444.3 5.0 reshape.372
  449.3 4.5 slice_bitcast_fusion
  455.5 2.9 copy.45
  458.4 2.2 copy.53
  460.6 9.5 %reduce-scatter.13.cloned.1.call-done = bf16[1,128,1024]{2,1,0:T(8,128)(2,1)} async-done(((bf16[1,1024,1024]{2,1,0:T(8,128)(2,1)}), bf16[1,128,1024]{2,1,0:T(8,128)(2,1)}) %reduce-scatter.13.cloned.1.call-update) | async-done | bytes 262160 | tf_op jit(solution)/shard_map/reduce_scatter | solution.py:71
  471.1 8.6 %all_gather.43 = bf16[1,256,1024]{2,1,0:T(8,128)(2,1)} all-gather(bf16[1,128,1024]{2,1,0:T(8,128)(2,1)S(1)} %add_convert_fusion.1), channel_id=1, replica_groups=mesh['shard'=4,'ctx'=4,'tp'=2] {'tp'}, dimensions={1}, use_global_device_ids=true | all-gather | bytes 786432 | tf_op jit(solution)/shard_map/all_gather | solution.py:245
  479.7 8.7 %all-gather.20.cloned.1.call-done = bf16[1024,512]{0,1:T(8,128)(2,1)} async-done(((bf16[256,512]{0,1:T(8,128)(2,1)}), bf16[1024,512]{0,1:T(8,128)(2,1)}) %all-gather.20.cloned.1.call-update) | async-done | bytes 1048592 | tf_op jit(solution)/shard_map/all_gather | solution.py:252
  496.3 2.0 copy.44
  (205 shorter events, 63.9 us)
Async XLA Ops:
  7.2 5.3 %copy-start.12 = (s32[1,1024]{1,0:T(1,128)S(1)}, s32[1,1024]{1,0:T(1,128)}, u32[]{:S(2)}) copy-start(s32[1,1024]{1,0:T(1,128)} %param.21) | copy-start | bytes 12292
  7.2 28.5 %all-gather.10.cloned.1.call-start = ((), (), s32[]{:S(2)}) async-start(), calls=%async_computation.6 | async-start | bytes 2621440 | tf_op jit(solution)/shard_map/all_gather | solution.py:113
  7.9 79.7 %all-gather.12.cloned.1.call-start = ((), (), s32[]{:S(2)}) async-start(), calls=%async_computation.7 | async-start | bytes 2949120 | tf_op jit(solution)/shard_map/all_gather | solution.py:117
  11.3 119.5 %reduce-scatter.7.cloned.1.call-start = ((), (), s32[]{:S(2)}) async-start(), calls=%async_computation.8 | async-start | bytes 2359296 | tf_op jit(solution)/shard_map/reduce_scatter | solution.py:71
  46.5 44.2 %copy-start.13 = (bf16[1024,2,64]{0,2,1:T(8,128)(2,1)}, bf16[1024,2,64]{0,2,1:T(8,128)(2,1)S(1)}, u32[]{:S(2)}) copy-start(bf16[1024,2,64]{0,2,1:T(8,128)(2,1)S(1)} %get-tuple-element.588) | copy-start | bytes 786436
  87.6 43.2 %copy-start.3 = (bf16[1,256,1024]{2,1,0:T(8,128)(2,1)S(1)}, bf16[1,256,1024]{2,1,0:T(8,128)(2,1)}, u32[]{:S(2)}) copy-start(bf16[1,256,1024]{2,1,0:T(8,128)(2,1)} %param.19) | copy-start | bytes 1572868
  87.6 43.2 %copy-start.15 = (f32[1024]{0:T(1024)S(1)}, f32[1024]{0:T(1024)}, u32[]{:S(2)}) copy-start(f32[1024]{0:T(1024)} %param.25) | copy-start | bytes 12292
  90.7 42.4 %copy-start.16 = (f32[1024]{0:T(1024)S(1)}, f32[1024]{0:T(1024)}, u32[]{:S(2)}) copy-start(f32[1024]{0:T(1024)} %param.26) | copy-start | bytes 12292
  90.7 42.4 %copy-start.17 = (f32[1024]{0:T(1024)S(1)}, f32[1024]{0:T(1024)}, u32[]{:S(2)}) copy-start(f32[1024]{0:T(1024)} %param.27) | copy-start | bytes 12292
  90.7 72.2 %all-gather.14.cloned.1.call-start = ((), (), s32[]{:S(2)}) async-start(), calls=%async_computation.9 | async-start | bytes 2359296 | tf_op jit(solution)/shard_map/all_gather | solution.py:67
  134.9 78.6 %reduce-scatter.9.cloned.1.call-start = ((), (), s32[]{:S(2)}) async-start(), calls=%async_computation.10 | async-start | bytes 2359296 | tf_op jit(solution)/shard_map/reduce_scatter | solution.py:71
  172.2 41.3 %copy-start.2 = (bf16[1,128,1024]{2,1,0:T(8,128)(2,1)S(1)}, bf16[1,128,1024]{2,1,0:T(8,128)(2,1)}, u32[]{:S(2)}) copy-start(bf16[1,128,1024]{2,1,0:T(8,128)(2,1)} %reduce-scatter.7.cloned.1.call-done) | copy-start | bytes 786436
  172.2 41.3 %copy-start.19 = (f32[1024]{0:T(1024)S(1)}, f32[1024]{0:T(1024)}, u32[]{:S(2)}) copy-start(f32[1024]{0:T(1024)} %param.31) | copy-start | bytes 12292
  172.2 42.8 %copy-start.10 = (bf16[1,256,1024]{2,1,0:T(8,128)(2,1)S(1)}, bf16[1,256,1024]{2,1,0:T(8,128)(2,1)}, u32[]{:S(2)}) copy-start(bf16[1,256,1024]{2,1,0:T(8,128)(2,1)} %param.20) | copy-start | bytes 1572868
  172.2 42.8 %copy-start.18 = (f32[1024]{0:T(1024)S(1)}, f32[1024]{0:T(1024)}, u32[]{:S(2)}) copy-start(f32[1024]{0:T(1024)} %param.32) | copy-start | bytes 12292
  172.2 43.1 %copy-start.20 = (f32[1024]{0:T(1024)S(1)}, f32[1024]{0:T(1024)}, u32[]{:S(2)}) copy-start(f32[1024]{0:T(1024)} %param.33) | copy-start | bytes 12292
  172.3 72.0 %all-gather.16.cloned.1.call-start = ((), (), s32[]{:S(2)}) async-start(), calls=%async_computation.11 | async-start | bytes 2359296 | tf_op jit(solution)/shard_map/all_gather | solution.py:67
  216.4 78.5 %reduce-scatter.11.cloned.1.call-start = ((), (), s32[]{:S(2)}) async-start(), calls=%async_computation.12 | async-start | bytes 2359296 | tf_op jit(solution)/shard_map/reduce_scatter | solution.py:71
  253.6 73.3 %all-gather.18.cloned.1.call-start = ((), (), s32[]{:S(2)}) async-start(), calls=%async_computation.13 | async-start | bytes 2359296 | tf_op jit(solution)/shard_map/all_gather | solution.py:67
  299.0 74.5 %reduce-scatter.17.cloned.1.call-start = ((), (), s32[]{:S(2)}) async-start(), calls=%async_computation.16 | async-start | bytes 2621440 | tf_op jit(solution)/shard_map/reduce_scatter | solution.py:251
  299.1 3.3 copy-start.22
  299.1 3.3 copy-start.25
  305.3 97.5 %reduce-scatter.15.cloned.1.call-start = ((), (), s32[]{:S(2)}) async-start(), calls=%async_computation.15 | async-start | bytes 1310720 | tf_op jit(solution)/shard_map/reduce_scatter | solution.py:251
  332.8 2.0 copy-start.9
  344.0 2.4 copy-start.21
  348.4 95.9 %all-gather.22.cloned.1.call-start = ((), (), s32[]{:S(2)}) async-start(), calls=%async_computation.18 | async-start | bytes 2621440 | tf_op jit(solution)/shard_map/all_gather | solution.py:252
  373.5 96.6 %reduce-scatter.13.cloned.1.call-start = ((), (), s32[]{:S(2)}) async-start(), calls=%async_computation.14 | async-start | bytes 2359296 | tf_op jit(solution)/shard_map/reduce_scatter | solution.py:71
  376.2 112.3 %all-gather.20.cloned.1.call-start = ((), (), s32[]{:S(2)}) async-start(), calls=%async_computation.17 | async-start | bytes 1310720 | tf_op jit(solution)/shard_map/all_gather | solution.py:252
  458.4 11.7 %copy-start.5 = (f32[1,128,1024]{2,1,0:T(8,128)S(1)}, f32[1,128,1024]{2,1,0:T(8,128)}, u32[]{:S(2)}) copy-start(f32[1,128,1024]{2,1,0:T(8,128)} %copy-done.4) | copy-start | bytes 1572868
  494.5 3.8 copy-start.6
  494.5 5.4 %copy-start.1 = (bf16[256,2048]{1,0:T(8,128)(2,1)S(1)}, bf16[256,2048]{1,0:T(8,128)(2,1)}, u32[]{:S(2)}) copy-start(bf16[256,2048]{1,0:T(8,128)(2,1)} %param.28) | copy-start | bytes 3145732
  496.3 2.8 copy-start.7
  (10 other events, 12.7 us)
Sparse Core Ops, SparseCore 0:
  9.6 25.2 all-gather.9
  37.0 50.5 all-gather.11
  91.5 39.2 reduce-scatter.6
  135.1 27.7 all-gather.13
  172.4 41.0 reduce-scatter.8
  216.5 27.7 all-gather.15
  253.7 41.0 reduce-scatter.10
  299.1 27.7 all-gather.17
  329.8 43.6 reduce-scatter.16
  376.2 26.4 reduce-scatter.14
  404.3 21.4 all-gather.21
  428.9 41.1 reduce-scatter.12
  471.6 16.7 all-gather.19
where the time goes:
time: 507 us; the launch traced here: 506 us
  waiting for transfers between devices  301 us (59%)
  blocking collectives  78 us (15%)
  matrix products  50.5 us (10%)
  local copies, waits for them, and re-layouts  40.4 us (8%)
  other arithmetic  20.5 us (4%)
  between operations  14.5 us (3%)
    reduce_scatter x4, waiting for transfers between devices, collect(): lax.psum_scatter(whole, GROUP, scatter_dimension=1, tiled=True)  132 us
    all_gather x3, waiting for transfers between devices, spread(): return lax.all_gather(part, GROUP, axis=1, tiled=True)  76.2 us
    reduce_scatter x2, waiting for transfers between devices, owned(): mean = lax.psum_scatter(part, 'shard', scatter_dimension=0, tiled=True)  42.8 us
    all_gather x1, waiting for transfers between devices, shards(): rest_full = lax.all_gather(rest_own, 'shard', axis=0, tiled=True)  40.8 us
    psum x1, blocking collectives, shards(): lax.psum(jnp.concatenate([bias_out_grad, gain_one_grad, shift_one_grad, b...  39.6 us
    all_gather x1, blocking collectives, shards(): qkv_full = lax.all_gather(qkv_own, 'shard', axis=0, tiled=True)  21.3 us
    dot_general x4, matrix products, dot(): return jnp.dot(left, right, preferred_element_type=jnp.float32)  14 us
    dot_general x4, matrix products, dot_t(): lax.dot_general(left, right, (((1,), (1,)), ((), ())), preferred_element_...  13.3 us
  transfers between devices with their start and end apart: 13, of which 11 were waited for; matrix products, arithmetic and copies ran while one was open for 13% of the time, Pallas kernels for 0%

commit v1 on v0

--- a/solution.py
+++ b/solution.py
@@ -109,12 +109,15 @@
         return lax.dynamic_slice_in_dim(array, ctx_at * size, size, axis)
 
     qkv_own = mine(w_qkv, cols, 2).transpose(1, 0, 2).reshape(owned_rows, 3 * cols)
-    qkv_full = lax.all_gather(qkv_own, "shard", axis=0, tiled=True)
     tokens_all = lax.all_gather(hidden_in, "ctx", axis=1, tiled=True).reshape(row_count, width)
     rest_own = jnp.concatenate(
         [mine(w_out, cols, 0).T, mine(w_up, units, 1), mine(w_down, units, 0).T], axis=1
     )
-    rest_full = lax.all_gather(rest_own, "shard", axis=0, tiled=True)
+    qkv_full, rest_full = jnp.split(
+        lax.all_gather(jnp.concatenate([qkv_own, rest_own], axis=1), "shard", axis=0, tiled=True),
+        [qkv_own.shape[1]],
+        axis=1,
+    )
     out_full = rest_full[:, :cols]
     up_full = rest_full[:, cols : cols + units]
     down_full = rest_full[:, cols + units :]

time: 507 us -> 531 us (1.047)
  waiting for transfers between devices: 301 us -> 347 us
  blocking collectives: 78 us -> 56.8 us
    all_gather x1, waiting for transfers between devices: 40.8 us -> 65.6 us  [shards(): lax.all_gather(jnp.concatenate([qkv_own, rest_own], axis=1), 'shard', axi...]
    all_gather x1 -> x0, blocking collectives: 21.3 us -> none  [shards(): qkv_full = lax.all_gather(qkv_own, 'shard', axis=0, tiled=True)]
    all_gather x1, waiting for transfers between devices: 0.02 us -> 20.9 us  [shards(): lax.all_gather(hidden_in, 'ctx', axis=1, tiled=True)]
  transfers between devices with their start and end apart: 13 -> 13, of which waited for: 11 -> 12; matrix products, arithmetic and copies ran while one was open for 13% -> 10% of each run, Pallas kernels for 0% -> 0%
where the time goes in v1:
time: 531 us; the launch traced here: 530 us
  waiting for transfers between devices  347 us (65%)
  blocking collectives  56.8 us (11%)
  matrix products  51.9 us (10%)
  local copies, waits for them, and re-layouts  39.4 us (7%)
  other arithmetic  19.5 us (4%)
  between operations  14.5 us (3%)
    reduce_scatter x4, waiting for transfers between devices, collect(): lax.psum_scatter(whole, GROUP, scatter_dimension=1, tiled=True)  131 us
    all_gather x3, waiting for transfers between devices, spread(): return lax.all_gather(part, GROUP, axis=1, tiled=True)  76.2 us
    all_gather x1, waiting for transfers between devices, shards(): lax.all_gather(jnp.concatenate([qkv_own, rest_own], axis=1), 'shard', axi...  65.6 us
    reduce_scatter x2, waiting for transfers between devices, owned(): mean = lax.psum_scatter(part, 'shard', scatter_dimension=0, tiled=True)  43.3 us
    psum x1, blocking collectives, shards(): lax.psum(jnp.concatenate([bias_out_grad, gain_one_grad, shift_one_grad, b...  39.7 us
    all_gather x1, waiting for transfers between devices, shards(): lax.all_gather(hidden_in, 'ctx', axis=1, tiled=True)  20.9 us
    dot_general x4, matrix products, dot_t(): lax.dot_general(left, right, (((1,), (1,)), ((), ())), preferred_element_...  14.4 us
    dot_general x4, matrix products, dot(): return jnp.dot(left, right, preferred_element_type=jnp.float32)  14.2 us
  transfers between devices with their start and end apart: 13, of which 12 were waited for; matrix products, arithmetic and copies ran while one was open for 10% of the time, Pallas kernels for 0%

profile of v1, /device:TPU:0, one launch (start us, length us, event | category | flops | bytes accessed | tf_op | source)
XLA Modules:
  0.0 530.0 jit_solution(18092988854492297396)
XLA Ops:
  14.0 20.9 %all-gather.12.cloned.1.call-done = bf16[1,1024,1024]{2,1,0:T(8,128)(2,1)} async-done(((bf16[1,256,1024]{2,1,0:T(8,128)(2,1)}), bf16[1,1024,1024]{2,1,0:T(8,128)(2,1)}) %all-gather.12.cloned.1.call-update) | async-done | bytes 2097168 | tf_op jit(solution)/shard_map/all_gather | solution.py:112
  34.9 65.6 %all-gather.10.cloned.1.call-done = bf16[1024,1536]{0,1:T(8,128)(2,1)} async-done(((bf16[256,1536]{0,1:T(8,128)(2,1)}), bf16[1024,1536]{0,1:T(8,128)(2,1)}) %all-gather.10.cloned.1.call-update) | async-done | bytes 3145744 | tf_op jit(solution)/shard_map/all_gather | solution.py:117
  100.4 2.9 add_convert_fusion
  103.6 7.9 %while.45 = (s32[]{:T(128)}, bf16[2,512,2,64]{1,3,2,0:T(8,128)(2,1)S(1)}, f32[2,2,512]{2,1,0:T(2,128)S(1)}, s32[2,512]{1,0:T(2,128)S(1)}, s32[1024]{0:T(1024)S(1...) while((s32[]{:T(128)}, ...), condition=%wide.region_3.4_spmd, body=%wide.region_0.3_spmd.sunk | while | flops 280567808 | bytes 15526005 | solution.py:146
  111.9 3.1 convert_bitcast_fusion.3
  115.0 39.4 %reduce-scatter.7.cloned.1.call-done = bf16[1,128,1024]{2,1,0:T(8,128)(2,1)} async-done(((bf16[1,1024,1024]{2,1,0:T(8,128)(2,1)}), bf16[1,128,1024]{2,1,0:T(8,128)(2,1)}) %reduce-scatter.7.cloned.1.call-update) | async-done | bytes 262160 | tf_op jit(solution)/shard_map/reduce_scatter | solution.py:71
  159.4 27.1 %all-gather.14.cloned.1.call-done = bf16[1,1024,1024]{2,1,0:T(8,128)(2,1)} async-done(((bf16[1,128,1024]{2,1,0:T(8,128)(2,1)}), bf16[1,1024,1024]{2,1,0:T(8,128)(2,1)}) %all-gather.14.cloned.1.call-update) | async-done | bytes 2097168 | tf_op jit(solution)/shard_map/all_gather | solution.py:67
  186.5 4.6 multiply_convert_fusion.1
  192.1 3.8 convert_bitcast_fusion.2
  195.9 41.2 %reduce-scatter.9.cloned.1.call-done = bf16[1,128,1024]{2,1,0:T(8,128)(2,1)} async-done(((bf16[1,1024,1024]{2,1,0:T(8,128)(2,1)}), bf16[1,128,1024]{2,1,0:T(8,128)(2,1)}) %reduce-scatter.9.cloned.1.call-update) | async-done | bytes 262160 | tf_op jit(solution)/shard_map/reduce_scatter | solution.py:71
  240.2 27.7 %all-gather.16.cloned.1.call-done = bf16[1,1024,1024]{2,1,0:T(8,128)(2,1)} async-done(((bf16[1,128,1024]{2,1,0:T(8,128)(2,1)}), bf16[1,1024,1024]{2,1,0:T(8,128)(2,1)}) %all-gather.16.cloned.1.call-update) | async-done | bytes 2097168 | tf_op jit(solution)/shard_map/all_gather | solution.py:67
  267.9 4.5 fusion.113
  273.3 3.8 convert_bitcast_fusion.1
  277.2 41.2 %reduce-scatter.11.cloned.1.call-done = bf16[1,128,1024]{2,1,0:T(8,128)(2,1)} async-done(((bf16[1,1024,1024]{2,1,0:T(8,128)(2,1)}), bf16[1,128,1024]{2,1,0:T(8,128)(2,1)}) %reduce-scatter.11.cloned.1.call-update) | async-done | bytes 262160 | tf_op jit(solution)/shard_map/reduce_scatter | solution.py:71
  322.7 3.3 fusion.72
  329.1 21.4 %all-gather.18.cloned.1.call-done = bf16[1,1024,1024]{2,1,0:T(8,128)(2,1)} async-done(((bf16[1,128,1024]{2,1,0:T(8,128)(2,1)}), bf16[1,1024,1024]{2,1,0:T(8,128)(2,1)}) %all-gather.18.cloned.1.call-update) | async-done | bytes 2097168 | tf_op jit(solution)/shard_map/all_gather | solution.py:67
  350.5 2.3 fusion.81
  353.5 11.8 %while.46 = (s32[]{:T(128)}, f32[1024,2,64]{0,2,1:T(8,128)S(1)}, f32[1024,2,64]{0,2,1:T(8,128)S(1)}, bf16[2,512,2,64]{1,3,2,0:T(8,128)(2,1)S(1)}, bf16[2,512,2,6...) while((s32[]{:T(128)}, f32[1024,2,64]{0,2,1:T(8,128)S(1)}, ...), condition=%wide.region_17.18_spmd.clone, body=%wide.region_15.17_spmd.clone.sunk | while | flops 683998208 | bytes 24283320 | solution.py:229
  366.0 2.2 fusion.84
  370.3 26.7 %reduce-scatter.17.cloned.1.call-done = bf16[256,1024]{0,1:T(8,128)(2,1)} async-done(((bf16[1024,1024]{0,1:T(8,128)(2,1)}), bf16[256,1024]{0,1:T(8,128)(2,1)}) %reduce-scatter.17.cloned.1.call-update) | async-done | bytes 524304 | tf_op jit(solution)/shard_map/reduce_scatter | solution.py:254
  397.1 3.8 convert_bitcast_fusion
  400.9 8.5 %all_gather.36 = bf16[1,256,1024]{2,1,0:T(8,128)(2,1)} all-gather(bf16[1,128,1024]{2,1,0:T(8,128)(2,1)S(1)} %get-tuple-element.297), channel_id=1, replica_groups=mesh['shard'=4,'ctx'=4,'tp'=2] {'tp'}, dimensions={1}, use_global_device_ids=true | all-gather | bytes 786432 | tf_op jit(solution)/shard_map/all_gather | solution.py:178
  409.7 16.6 %reduce-scatter.15.cloned.1.call-done = bf16[256,512]{0,1:T(8,128)(2,1)} async-done(((bf16[1024,512]{0,1:T(8,128)(2,1)}), bf16[256,512]{0,1:T(8,128)(2,1)}) %reduce-scatter.15.cloned.1.call-update) | async-done | bytes 262160 | tf_op jit(solution)/shard_map/reduce_scatter | solution.py:254
  426.3 39.7 %psum.7 = f32[12288]{0:T(1024)S(1)} all-reduce(f32[12288]{0:T(1024)S(1)} %constant_dynamic-update-slice_fusion), channel_id=1, replica_groups=mesh['shard'=4,'ctx'=4,'tp'=2] {'shard','ctx','tp'}, use_global_device_ids=true, to_apply=%region_28.29 | all-reduce | flops 12288 | bytes 98304 | tf_op jit(solution)/shard_map/psum | solution.py:271
  467.9 5.0 reshape.372
  472.9 4.5 slice_bitcast_fusion
  479.1 2.9 copy.46
  482.0 2.2 copy.53
  484.2 9.5 %reduce-scatter.13.cloned.1.call-done = bf16[1,128,1024]{2,1,0:T(8,128)(2,1)} async-done(((bf16[1,1024,1024]{2,1,0:T(8,128)(2,1)}), bf16[1,128,1024]{2,1,0:T(8,128)(2,1)}) %reduce-scatter.13.cloned.1.call-update) | async-done | bytes 262160 | tf_op jit(solution)/shard_map/reduce_scatter | solution.py:71
  494.7 8.6 %all_gather.39 = bf16[1,256,1024]{2,1,0:T(8,128)(2,1)} all-gather(bf16[1,128,1024]{2,1,0:T(8,128)(2,1)S(1)} %add_convert_fusion.1), channel_id=1, replica_groups=mesh['shard'=4,'ctx'=4,'tp'=2] {'tp'}, dimensions={1}, use_global_device_ids=true | all-gather | bytes 786432 | tf_op jit(solution)/shard_map/all_gather | solution.py:248
  503.3 8.7 %all-gather.20.cloned.1.call-done = bf16[1024,512]{0,1:T(8,128)(2,1)} async-done(((bf16[256,512]{0,1:T(8,128)(2,1)}), bf16[1024,512]{0,1:T(8,128)(2,1)}) %all-gather.20.cloned.1.call-update) | async-done | bytes 1048592 | tf_op jit(solution)/shard_map/all_gather | solution.py:255
  519.9 2.0 copy.45
  (188 shorter events, 61.9 us)
Async XLA Ops:
  7.2 1.9 copy-start
  7.2 27.7 %all-gather.12.cloned.1.call-start = ((), (), s32[]{:S(2)}) async-start(), calls=%async_computation.7 | async-start | bytes 2621440 | tf_op jit(solution)/shard_map/all_gather | solution.py:112
  7.9 92.5 %all-gather.10.cloned.1.call-start = ((), (), s32[]{:S(2)}) async-start(), calls=%async_computation.6 | async-start | bytes 3932160 | tf_op jit(solution)/shard_map/all_gather | solution.py:117
  9.1 3.6 copy-start.9
  12.1 142.3 %reduce-scatter.7.cloned.1.call-start = ((), (), s32[]{:S(2)}) async-start(), calls=%async_computation.8 | async-start | bytes 2359296 | tf_op jit(solution)/shard_map/reduce_scatter | solution.py:71
  111.8 42.6 %copy-start.3 = (bf16[1,256,1024]{2,1,0:T(8,128)(2,1)S(1)}, bf16[1,256,1024]{2,1,0:T(8,128)(2,1)}, u32[]{:S(2)}) copy-start(bf16[1,256,1024]{2,1,0:T(8,128)(2,1)} %param.19) | copy-start | bytes 1572868
  111.9 42.6 %copy-start.10 = (f32[1024]{0:T(1024)S(1)}, f32[1024]{0:T(1024)}, u32[]{:S(2)}) copy-start(f32[1024]{0:T(1024)} %param.25) | copy-start | bytes 12292
  114.9 41.8 %copy-start.11 = (f32[1024]{0:T(1024)S(1)}, f32[1024]{0:T(1024)}, u32[]{:S(2)}) copy-start(f32[1024]{0:T(1024)} %param.26) | copy-start | bytes 12292
  114.9 41.8 %copy-start.12 = (f32[1024]{0:T(1024)S(1)}, f32[1024]{0:T(1024)}, u32[]{:S(2)}) copy-start(f32[1024]{0:T(1024)} %param.27) | copy-start | bytes 12292
  115.0 71.5 %all-gather.14.cloned.1.call-start = ((), (), s32[]{:S(2)}) async-start(), calls=%async_computation.9 | async-start | bytes 2359296 | tf_op jit(solution)/shard_map/all_gather | solution.py:67
  158.6 78.6 %reduce-scatter.9.cloned.1.call-start = ((), (), s32[]{:S(2)}) async-start(), calls=%async_computation.10 | async-start | bytes 2359296 | tf_op jit(solution)/shard_map/reduce_scatter | solution.py:71
  195.8 41.3 %copy-start.2 = (bf16[1,128,1024]{2,1,0:T(8,128)(2,1)S(1)}, bf16[1,128,1024]{2,1,0:T(8,128)(2,1)}, u32[]{:S(2)}) copy-start(bf16[1,128,1024]{2,1,0:T(8,128)(2,1)} %reduce-scatter.7.cloned.1.call-done) | copy-start | bytes 786436
  195.9 41.3 %copy-start.14 = (f32[1024]{0:T(1024)S(1)}, f32[1024]{0:T(1024)}, u32[]{:S(2)}) copy-start(f32[1024]{0:T(1024)} %param.31) | copy-start | bytes 12292
  195.9 42.8 %copy-start.8 = (bf16[1,256,1024]{2,1,0:T(8,128)(2,1)S(1)}, bf16[1,256,1024]{2,1,0:T(8,128)(2,1)}, u32[]{:S(2)}) copy-start(bf16[1,256,1024]{2,1,0:T(8,128)(2,1)} %param.20) | copy-start | bytes 1572868
  195.9 42.8 %copy-start.13 = (f32[1024]{0:T(1024)S(1)}, f32[1024]{0:T(1024)}, u32[]{:S(2)}) copy-start(f32[1024]{0:T(1024)} %param.32) | copy-start | bytes 12292
  195.9 43.1 %copy-start.15 = (f32[1024]{0:T(1024)S(1)}, f32[1024]{0:T(1024)}, u32[]{:S(2)}) copy-start(f32[1024]{0:T(1024)} %param.33) | copy-start | bytes 12292
  195.9 72.0 %all-gather.16.cloned.1.call-start = ((), (), s32[]{:S(2)}) async-start(), calls=%async_computation.11 | async-start | bytes 2359296 | tf_op jit(solution)/shard_map/all_gather | solution.py:67
  239.9 78.5 %reduce-scatter.11.cloned.1.call-start = ((), (), s32[]{:S(2)}) async-start(), calls=%async_computation.12 | async-start | bytes 2359296 | tf_op jit(solution)/shard_map/reduce_scatter | solution.py:71
  272.4 1.0 copy-start.19
  277.2 73.3 %all-gather.18.cloned.1.call-start = ((), (), s32[]{:S(2)}) async-start(), calls=%async_computation.13 | async-start | bytes 2359296 | tf_op jit(solution)/shard_map/all_gather | solution.py:67
  322.6 74.5 %reduce-scatter.17.cloned.1.call-start = ((), (), s32[]{:S(2)}) async-start(), calls=%async_computation.16 | async-start | bytes 2621440 | tf_op jit(solution)/shard_map/reduce_scatter | solution.py:254
  322.6 3.3 copy-start.17
  322.6 3.3 copy-start.20
  328.8 97.5 %reduce-scatter.15.cloned.1.call-start = ((), (), s32[]{:S(2)}) async-start(), calls=%async_computation.15 | async-start | bytes 1310720 | tf_op jit(solution)/shard_map/reduce_scatter | solution.py:254
  365.9 2.4 copy-start.16
  370.3 97.6 %all-gather.22.cloned.1.call-start = ((), (), s32[]{:S(2)}) async-start(), calls=%async_computation.18 | async-start | bytes 2621440 | tf_op jit(solution)/shard_map/all_gather | solution.py:255
  397.1 96.6 %reduce-scatter.13.cloned.1.call-start = ((), (), s32[]{:S(2)}) async-start(), calls=%async_computation.14 | async-start | bytes 2359296 | tf_op jit(solution)/shard_map/reduce_scatter | solution.py:71
  400.9 111.2 %all-gather.20.cloned.1.call-start = ((), (), s32[]{:S(2)}) async-start(), calls=%async_computation.17 | async-start | bytes 1310720 | tf_op jit(solution)/shard_map/all_gather | solution.py:255
  482.0 11.7 %copy-start.5 = (f32[1,128,1024]{2,1,0:T(8,128)S(1)}, f32[1,128,1024]{2,1,0:T(8,128)}, u32[]{:S(2)}) copy-start(f32[1,128,1024]{2,1,0:T(8,128)} %copy-done.4) | copy-start | bytes 1572868
  518.1 3.8 copy-start.6
  518.1 5.4 %copy-start.1 = (bf16[256,2048]{1,0:T(8,128)(2,1)S(1)}, bf16[256,2048]{1,0:T(8,128)(2,1)}, u32[]{:S(2)}) copy-start(bf16[256,2048]{1,0:T(8,128)(2,1)} %param.28) | copy-start | bytes 3145732
  519.9 2.8 copy-start.7
  (2 other events, 1.8 us)
Sparse Core Ops, SparseCore 0:
  9.6 25.2 all-gather.11
  37.0 63.3 all-gather.9
  115.1 39.2 reduce-scatter.6
  158.7 27.7 all-gather.13
  196.0 41.0 reduce-scatter.8
  240.1 27.7 all-gather.15
  277.3 41.0 reduce-scatter.10
  322.7 27.7 all-gather.17
  353.4 43.6 reduce-scatter.16
  399.7 26.4 reduce-scatter.14
  427.8 21.4 all-gather.21
  452.5 41.1 reduce-scatter.12
  495.2 16.7 all-gather.19
